TPU v7x, 128 devices: a whole 4x4x4 slice. The times are simulated.
128 devices in a mesh: row: 8 (over x, z_hi), col: 16 (over y, z_lo, core).
Axes of the slice: x: 4, y: 4, z: 4 (z_hi: 2, z_lo: 2; z = z_hi * 2 + z_lo), core: 2. Of those that a mesh axis runs over, the one named last changes fastest.
Arguments:
- residual: bfloat16 [256, 5120], P('row', 'col'), may hold values from -6 to 6
- attn_gain: float32 [5120], P('col'), may hold values from 0.1 to 1.9
- w_query: bfloat16 [5120, 5120], P('col', 'row'), may hold values from -0.078125 to 0.078125
- w_key: bfloat16 [5120, 1024], P('col', 'row'), may hold values from -0.078125 to 0.078125
- w_value: bfloat16 [5120, 1024], P('col', 'row'), may hold values from -0.078125 to 0.078125
- w_out: bfloat16 [5120, 5120], P('row', 'col'), may hold values from -0.078125 to 0.078125
- mlp_gain: float32 [5120], P('col'), may hold values from 0.1 to 1.9
- w_gate: bfloat16 [2, 5120, 13824], P(None, 'col', 'row'), may hold values from -0.078125 to 0.078125
- w_up: bfloat16 [2, 5120, 13824], P(None, 'col', 'row'), may hold values from -0.078125 to 0.078125
- w_down: bfloat16 [2, 13824, 5120], P(None, 'row', 'col'), may hold values from -0.0546875 to 0.0546875
- final_gain: float32 [5120], P('col'), may hold values from 0.1 to 1.9
- w_head: bfloat16 [5120, 81920], P(None, ('row', 'col')), may hold values from -32 to 32
- seq_lengths: int32 [8], replicated, may hold values from 1 to 64, 256 in all
- targets: int32 [256], replicated, may hold values from 0 to 81919
Outputs:
- seq_diff: float32 [8], replicated
Inputs may be any that keep to these rules, and one draw needn't show every extreme that they name: `seq_lengths`: the lengths sum to 256 and the largest is exactly 64.
All inputs are finite; a program needn't handle non-finite values.
Results may differ from a plain program's by a relative error of at most 0.02.
Values may be sent and summed in bfloat16 or wider, within the bound.
A program may use at most 64 MiB of HBM per device.

v0:
```python
import jax
import jax.numpy as jnp
from jax import lax
from jax.sharding import PartitionSpec as P

D = 5120
HEAD_DIM = 128
SEQS = 8
EPSILON = 1e-06
ROPE_BASE = 1000000.0
MASKED = -1e30


def sequence_layout(seq_lengths, token_index):
    ends_at = jnp.cumsum(seq_lengths)
    before = ends_at[None, :] <= token_index[:, None]
    segment = jnp.sum(before.astype(jnp.int32), axis=1)
    starts_at = jnp.sum(jnp.where(before, seq_lengths[None, :], 0), axis=1)
    return (segment, (token_index - starts_at).astype(jnp.float32))


def angles_for(positions, head_width):
    exponent = jnp.arange(head_width // 2, dtype=jnp.float32) * 2.0 / head_width
    frequency = ROPE_BASE ** (-exponent)
    return positions[:, None] * frequency[None, :]


def rotate(features, angles):
    half_width = features.shape[-1] // 2
    lower_half = features[..., :half_width]
    upper_half = features[..., half_width:]
    cosine = jnp.cos(angles)[:, None, :]
    sine_part = jnp.sin(angles)[:, None, :]
    return jnp.concatenate(
        [
            lower_half * cosine - upper_half * sine_part,
            upper_half * cosine + lower_half * sine_part,
        ],
        axis=-1,
    )


def rms_local(features, gain_vector):
    squares = jnp.sum(features * features, axis=1)
    grand_total = lax.psum(squares, "col")
    return features * lax.rsqrt(grand_total / D + EPSILON)[:, None] * gain_vector[None, :]


def feed_forward(mlp_input, gate_up, down_weight):
    ff_local = down_weight.shape[0]
    row_block = mlp_input
    summed = lax.psum_scatter(
        jnp.dot(row_block, gate_up, preferred_element_type=jnp.float32),
        "col",
        scatter_dimension=0,
        tiled=True,
    )
    hidden = (jax.nn.silu(summed[:, :ff_local]) * summed[:, ff_local:]).astype(jnp.bfloat16)
    hidden_all = lax.all_gather(hidden, "col", axis=0, tiled=True)
    row_block = hidden_all
    return lax.psum_scatter(
        jnp.dot(row_block, down_weight, preferred_element_type=jnp.float32),
        "row",
        scatter_dimension=0,
        tiled=True,
    )


def per_device(
    residual,
    attn_gain,
    w_query,
    w_key,
    w_value,
    w_out,
    mlp_gain,
    w_gate,
    w_up,
    w_down,
    final_gain,
    w_head,
    seq_lengths,
    targets,
):
    row_count = lax.axis_size("row")
    col_count = lax.axis_size("col")
    row_index = lax.axis_index("row")
    col_index = lax.axis_index("col")
    local_rows = residual.shape[0]
    total_tokens = local_rows * row_count
    query_heads = w_query.shape[1] // HEAD_DIM
    kv_local = w_key.shape[1] // HEAD_DIM
    group_size = query_heads // kv_local
    query_width = query_heads * HEAD_DIM
    key_width = kv_local * HEAD_DIM
    stream_in = residual.astype(jnp.float32)
    normed = rms_local(stream_in, attn_gain).astype(jnp.bfloat16)
    gathered = lax.all_gather(normed, "row", axis=0, tiled=True)
    w_joint = jnp.concatenate([w_query, w_key, w_value], axis=1)
    joint_part = jnp.dot(gathered, w_joint, preferred_element_type=jnp.float32)
    joint_sums = lax.psum(joint_part, "col")
    token_index = jnp.arange(total_tokens, dtype=jnp.int32)
    segment, positions = sequence_layout(seq_lengths, token_index)
    angles = angles_for(positions, HEAD_DIM)
    queries = rotate(
        joint_sums[:, :query_width].reshape(total_tokens, query_heads, HEAD_DIM), angles
    ).astype(jnp.bfloat16)
    keys_all = rotate(
        joint_sums[:, query_width : query_width + key_width].reshape(
            total_tokens, kv_local, HEAD_DIM
        ),
        angles,
    ).astype(jnp.bfloat16)
    values_all = (
        joint_sums[:, query_width + key_width :]
        .astype(jnp.bfloat16)
        .reshape(total_tokens, kv_local, HEAD_DIM)
    )
    grouped = queries.reshape(total_tokens, kv_local, group_size, HEAD_DIM)
    block_rows = min(512, total_tokens)
    block_count = total_tokens // block_rows

    def attend_block(block_start):
        block_index = block_start + jnp.arange(block_rows, dtype=jnp.int32)
        scores = jnp.einsum(
            "qhgd,khd->hgqk", grouped, keys_all, preferred_element_type=jnp.float32
        ) * HEAD_DIM ** (-0.5)
        allowed = (segment[:, None] == segment[None, :]) & (
            token_index[None, :] <= block_index[:, None]
        )
        scores = jnp.where(allowed[None, None], scores, MASKED)
        top_value = jnp.max(scores, axis=-1, keepdims=True)
        weights = jnp.exp(scores - top_value)
        weights = (weights / jnp.sum(weights, axis=-1, keepdims=True)).astype(jnp.bfloat16)
        result = jnp.einsum(
            "hgqk,khd->qhgd", weights, values_all, preferred_element_type=jnp.float32
        )
        return result.astype(jnp.bfloat16).reshape(block_rows, query_width)

    block_starts = jnp.arange(block_count, dtype=jnp.int32) * block_rows
    attn_all = lax.map(attend_block, block_starts).reshape(total_tokens, query_width)
    projected = lax.psum_scatter(
        jnp.dot(attn_all, w_out, preferred_element_type=jnp.float32),
        "row",
        scatter_dimension=0,
        tiled=True,
    )
    stream = lax.optimization_barrier((stream_in + projected).astype(jnp.bfloat16))
    stream_f = stream.astype(jnp.float32)
    mlp_in = rms_local(stream_f, mlp_gain).astype(jnp.bfloat16)
    mlp_input = lax.all_gather(mlp_in, "row", axis=0, tiled=True)
    outputs = []
    for member in range(2):
        gate_up = jnp.concatenate([w_gate[member], w_up[member]], axis=1)
        outputs.append(stream_f + feed_forward(mlp_input, gate_up, w_down[member]))
    pair_sums = lax.psum(
        (jnp.sum(outputs[0] * outputs[0], axis=1), jnp.sum(outputs[1] * outputs[1], axis=1)), "col"
    )
    policy_final = (
        outputs[0] * lax.rsqrt(pair_sums[0] / D + EPSILON)[:, None] * final_gain[None, :]
    ).astype(jnp.bfloat16)
    refer_final = (
        outputs[1] * lax.rsqrt(pair_sums[1] / D + EPSILON)[:, None] * final_gain[None, :]
    ).astype(jnp.bfloat16)
    wide_pair = (
        lax.all_gather(policy_final, "col", axis=1, tiled=True),
        lax.all_gather(refer_final, "col", axis=1, tiled=True),
    )
    policy_all, refer_all = (
        lax.all_gather(wide_pair[0], "row", axis=0, tiled=True),
        lax.all_gather(wide_pair[1], "row", axis=0, tiled=True),
    )
    vocab_local = w_head.shape[1]
    vocab_start = (row_index * col_count + col_index) * vocab_local
    vocab_ids = vocab_start + jnp.arange(vocab_local, dtype=jnp.int32)
    target_hits = targets[:, None] == vocab_ids[None, :]

    def local_stats(final_all):
        logits = jnp.dot(final_all, w_head, preferred_element_type=jnp.float32)
        local_top = jnp.max(logits, axis=1)
        local_total = jnp.sum(jnp.exp(logits - local_top[:, None]), axis=1)
        picked = jnp.sum(jnp.where(target_hits, logits, 0.0), axis=1)
        return (local_top, local_total, picked)

    policy_top, policy_total, policy_picked = local_stats(policy_all)
    refer_top, refer_total, refer_picked = local_stats(refer_all)
    top_policy, top_refer = lax.pmax((policy_top, refer_top), ("row", "col"))
    vocab_sums = lax.psum(
        (
            policy_total * jnp.exp(policy_top - top_policy),
            refer_total * jnp.exp(refer_top - top_refer),
            policy_picked,
            refer_picked,
        ),
        ("row", "col"),
    )
    policy_logprob = vocab_sums[2] - (top_policy + jnp.log(vocab_sums[0]))
    refer_logprob = vocab_sums[3] - (top_refer + jnp.log(vocab_sums[1]))
    difference = policy_logprob - refer_logprob
    one_hot = (segment[:, None] == jnp.arange(SEQS, dtype=jnp.int32)[None, :]).astype(jnp.float32)
    seq_sums = jnp.dot(difference, one_hot, precision=lax.Precision.HIGHEST)
    return seq_sums / seq_lengths.astype(jnp.float32)


def solution(mesh):
    placed = (
        P("row", "col"),
        P("col"),
        P("col", "row"),
        P("col", "row"),
        P("col", "row"),
        P("row", "col"),
        P("col"),
        P(None, "col", "row"),
        P(None, "col", "row"),
        P(None, "row", "col"),
        P("col"),
        P(None, ("row", "col")),
        P(),
        P(),
    )
    return jax.shard_map(per_device, mesh=mesh, in_specs=placed, out_specs=P(), check_vma=False)
```

profile of v0, /device:TPU:1, one launch (start us, length us, event | category | flops | bytes accessed | tf_op | source)
XLA Modules:
  0.0 926.4 jit_solution(10719453309221844499)
XLA Ops:
  6.5 0.9 fusion.48
  7.5 28.6 %psum.63 = f32[32]{0:T(128)S(1)} all-reduce(f32[32]{0:T(128)S(1)} %fusion.48), channel_id=1, replica_groups=mesh['row'=8,'col'=16] {'col'}, use_global_device_ids=true, to_apply=%region_1.0 | all-reduce | flops 32 | bytes 256 | tf_op jit(solution)/shard_map/psum | solution.py:45
  36.1 0.8 fusion.50
  36.9 28.5 %all_gather.24 = bf16[256,320]{1,0:T(8,128)(2,1)S(1)} all-gather(bf16[32,320]{1,0:T(8,128)(2,1)S(1)} %fusion.50), channel_id=1, replica_groups=mesh['row'=8,'col'=16] {'row'}, dimensions={0}, use_global_device_ids=true | all-gather | bytes 184320 | tf_op jit(solution)/shard_map/all_gather | solution.py:98
  65.4 2.5 fusion.21
  68.3 0.5 multiply_cosine_fusion
  68.9 126.3 %all-reduce.5.cloned.1.call-done = f32[256,896]{1,0:T(8,128)} async-done(((f32[256,896]{1,0:T(8,128)}), f32[256,896]{1,0:T(8,128)}) %all-reduce.5.cloned.1.call-update) | async-done | bytes 917520 | tf_op jit(solution)/shard_map/psum | solution.py:101
  195.2 1.1 slice.73
  196.3 0.2 copy.33
  196.6 0.2 copy.43
  196.9 0.2 copy.44
  197.1 0.9 slice_bitcast_fusion.4
  198.0 0.6 fusion.47
  198.8 0.5 fusion.62
  199.4 1.3 convolution_convert_fusion
  200.7 1.1 fusion.65
  202.0 4.0 slice_bitcast_fusion.2
  206.0 66.2 %reduce-scatter.6.cloned.1.call-done = f32[32,320]{1,0:T(8,128)} async-done(((f32[256,320]{1,0:T(8,128)}), f32[32,320]{1,0:T(8,128)}) %reduce-scatter.6.cloned.1.call-update) | async-done | bytes 40976 | tf_op jit(solution)/shard_map/reduce_scatter | solution.py:142
  272.1 0.8 fusion.51
  273.0 29.0 %psum.65 = f32[32]{0:T(128)S(1)} all-reduce(f32[32]{0:T(128)S(1)} %fusion.52), channel_id=1, replica_groups=mesh['row'=8,'col'=16] {'col'}, use_global_device_ids=true, to_apply=%region_10.11 | all-reduce | flops 32 | bytes 256 | tf_op jit(solution)/shard_map/psum | solution.py:45
  302.2 28.0 %all_gather.25 = bf16[256,320]{1,0:T(8,128)(2,1)S(1)} all-gather(bf16[32,320]{1,0:T(8,128)(2,1)S(1)} %fusion.54), channel_id=1, replica_groups=mesh['row'=8,'col'=16] {'row'}, dimensions={0}, use_global_device_ids=true | all-gather | bytes 184320 | tf_op jit(solution)/shard_map/all_gather | solution.py:151
  330.2 4.5 fusion.4
  334.8 2.9 fusion
  337.7 63.7 %reduce-scatter.12.cloned.1.call-done = f32[16,3456]{1,0:T(8,128)} async-done(((f32[256,3456]{1,0:T(8,128)}), f32[16,3456]{1,0:T(8,128)}) %reduce-scatter.12.cloned.1.call-update) | async-done | bytes 221200 | tf_op jit(solution)/shard_map/reduce_scatter | solution.py:52
  401.4 1.1 fusion.39
  402.5 24.7 %all_gather.29 = bf16[256,1728]{1,0:T(8,128)(2,1)S(1)} all-gather(bf16[16,1728]{1,0:T(8,128)(2,1)S(1)} %fusion.39), channel_id=1, replica_groups=mesh['row'=8,'col'=16] {'col'}, dimensions={0}, use_global_device_ids=true | all-gather | bytes 940032 | tf_op jit(solution)/shard_map/all_gather | solution.py:59
  427.2 1.4 fusion.11
  428.7 42.0 %reduce-scatter.8.cloned.1.call-done = f32[16,3456]{1,0:T(8,128)} async-done(((f32[256,3456]{1,0:T(8,128)}), f32[16,3456]{1,0:T(8,128)}) %reduce-scatter.8.cloned.1.call-update) | async-done | bytes 221200 | tf_op jit(solution)/shard_map/reduce_scatter | solution.py:52
  470.6 1.1 fusion.40
  471.7 21.1 %all_gather.26 = bf16[256,1728]{1,0:T(8,128)(2,1)S(1)} all-gather(bf16[16,1728]{1,0:T(8,128)(2,1)S(1)} %fusion.40), channel_id=1, replica_groups=mesh['row'=8,'col'=16] {'col'}, dimensions={0}, use_global_device_ids=true | all-gather | bytes 940032 | tf_op jit(solution)/shard_map/all_gather | solution.py:59
  492.8 1.4 fusion.13
  494.2 50.7 %reduce-scatter.14.cloned.1.call-done = f32[32,320]{1,0:T(8,128)} async-done(((f32[256,320]{1,0:T(8,128)}), f32[32,320]{1,0:T(8,128)}) %reduce-scatter.14.cloned.1.call-update) | async-done | bytes 40976 | tf_op jit(solution)/shard_map/reduce_scatter | solution.py:61
  545.0 74.0 %reduce-scatter.10.cloned.1.call-done = f32[32,320]{1,0:T(8,128)} async-done(((f32[256,320]{1,0:T(8,128)}), f32[32,320]{1,0:T(8,128)}) %reduce-scatter.10.cloned.1.call-update) | async-done | bytes 40976 | tf_op jit(solution)/shard_map/reduce_scatter | solution.py:61
  618.9 0.9 multiply_reduce_fusion.1
  619.9 29.1 %all-reduce.2 = (f32[32]{0:T(128)S(1)}, f32[32]{0:T(128)S(1)}) all-reduce(f32[32]{0:T(128)S(1)} %get-tuple-element.30, f32[32]{0:T(128)S(1)} %get-tuple-element.28), channel_id=1, replica_groups=mesh['row'=8,'col'=16] {'col'}, use_global_device_ids=true, to_apply=%region_24.25 | all-reduce | flops 64 | bytes 512 | tf_op jit(solution)/shard_map/psum | solution.py:156
  649.0 0.9 fusion.55
  649.9 18.1 %all-gather = bf16[16,320,32]{1,2,0:T(8,128)(2,1)S(1)} all-gather(bf16[1,320,32]{1,2,0:T(8,128)(2,1)S(1)} %get-tuple-element.52), channel_id=1, replica_groups=mesh['row'=8,'col'=16] {'col'}, dimensions={0}, use_global_device_ids=true | all-gather | bytes 348160 | tf_op jit(solution)/shard_map/all_gather | solution.py:166
  668.1 1.0 reshape.255
  669.2 19.3 %all-gather.1 = bf16[16,320,32]{1,2,0:T(8,128)(2,1)S(1)} all-gather(bf16[1,320,32]{1,2,0:T(8,128)(2,1)S(1)} %get-tuple-element.53), channel_id=1, replica_groups=mesh['row'=8,'col'=16] {'col'}, dimensions={0}, use_global_device_ids=true | all-gather | bytes 348160 | tf_op jit(solution)/shard_map/all_gather | solution.py:167
  688.6 1.0 reshape.257
  689.6 35.1 %all-gather.5.cloned.1.call-done = bf16[256,5120]{1,0:T(8,128)(2,1)} async-done(((bf16[32,5120]{1,0:T(8,128)(2,1)}), bf16[256,5120]{1,0:T(8,128)(2,1)}) %all-gather.5.cloned.1.call-update) | async-done | bytes 2621456 | tf_op jit(solution)/shard_map/all_gather | solution.py:170
  724.8 5.9 fusion.63
  730.7 54.1 %all-gather.7.cloned.1.call-done = bf16[256,5120]{1,0:T(8,128)(2,1)} async-done(((bf16[32,5120]{1,0:T(8,128)(2,1)}), bf16[256,5120]{1,0:T(8,128)(2,1)}) %all-gather.7.cloned.1.call-update) | async-done | bytes 2621456 | tf_op jit(solution)/shard_map/all_gather | solution.py:171
  784.9 5.9 fusion.64
  790.8 65.0 %all-reduce.1 = (f32[256]{0:T(256)S(1)}, f32[256]{0:T(256)S(1)}) all-reduce(f32[256]{0:T(256)S(1)} %get-tuple-element.62, f32[256]{0:T(256)S(1)} %get-tuple-element.60), channel_id=1, replica_groups=mesh['row'=8,'col'=16] {'row','col'}, use_global_device_ids=true, to_apply=%region_28.29 | all-reduce | flops 512 | bytes 4096 | tf_op jit(solution)/shard_map/pmax | solution.py:187
  855.8 0.5 exponential_reduce_fusion.1
  856.3 62.5 %all-reduce = (f32[256]{0:T(256)S(1)}, f32[256]{0:T(256)S(1)}, f32[256]{0:T(256)S(1)}, f32[256]{0:T(256)S(1)}) all-reduce(f32[256]{0:T(256)S(1)} %get-tuple-element.54, f32[256]{0:T(256)S(1)} %exponential_multiply_fusion, f32[256]{0:T(256)S(1)} %get-tuple-element.18, ...), channel_id=1, replica_groups=mesh['row'=8,'col'=16] {'row','col'}, use_global_device_ids=true, to_apply=%region_26.27 | all-reduce | flops 1024 | bytes 8192 | tf_op jit(solution)/shard_map/psum | solution.py:188
  918.8 0.8 fusion.17
  (50 shorter events, 1.8 us)
Async XLA Ops:
  6.5 194.2 %copy-start = (bf16[640,320]{0,1:T(8,128)(2,1)S(1)}, bf16[640,320]{0,1:T(8,128)(2,1)}, u32[]{:S(2)}) copy-start(bf16[640,320]{0,1:T(8,128)(2,1)} %param.19) | copy-start | bytes 1228804
  6.5 61.4 %copy-start.5 = (s32[8]{0:T(128)S(1)}, s32[8]{0:T(128)}, u32[]{:S(2)}) copy-start(s32[8]{0:T(128)} %param.26) | copy-start | bytes 100
  6.5 188.7 %all-reduce.5.cloned.1.call-start = ((), (), s32[]{:S(2)}) async-start(), calls=%async_computation.5 | async-start | bytes 1835008 | tf_op jit(solution)/shard_map/psum | solution.py:101
  67.9 204.2 %reduce-scatter.6.cloned.1.call-start = ((), (), s32[]{:S(2)}) async-start(), calls=%async_computation.6 | async-start | bytes 442368 | tf_op jit(solution)/shard_map/reduce_scatter | solution.py:142
  201.9 70.2 %copy-start.1 = (bf16[32,320]{1,0:T(8,128)(2,1)S(1)}, bf16[32,320]{1,0:T(8,128)(2,1)}, u32[]{:S(2)}) copy-start(bf16[32,320]{1,0:T(8,128)(2,1)} %param.14) | copy-start | bytes 61444
  201.9 100.2 %copy-start.3 = (f32[320]{0:T(512)S(1)}, f32[320]{0:T(512)}, u32[]{:S(2)}) copy-start(f32[320]{0:T(512)} %param.20) | copy-start | bytes 3844
  201.9 199.5 %reduce-scatter.12.cloned.1.call-start = ((), (), s32[]{:S(2)}) async-start(), calls=%async_computation.10 | async-start | bytes 3760128 | tf_op jit(solution)/shard_map/reduce_scatter | solution.py:52
  334.7 135.9 %reduce-scatter.8.cloned.1.call-start = ((), (), s32[]{:S(2)}) async-start(), calls=%async_computation.7 | async-start | bytes 3760128 | tf_op jit(solution)/shard_map/reduce_scatter | solution.py:52
  337.6 89.5 %copy-start.6 = (bf16[2,1728,320]{1,2,0:T(8,128)(2,1)S(1)}, bf16[2,1728,320]{1,2,0:T(8,128)(2,1)}, u32[]{:S(2)}) copy-start(bf16[2,1728,320]{1,2,0:T(8,128)(2,1)} %param.23) | copy-start | bytes 6635524
  337.7 207.3 %reduce-scatter.14.cloned.1.call-start = ((), (), s32[]{:S(2)}) async-start(), calls=%async_computation.11 | async-start | bytes 442368 | tf_op jit(solution)/shard_map/reduce_scatter | solution.py:61
  428.6 220.3 %copy-start.2 = (f32[320]{0:T(512)S(1)}, f32[320]{0:T(512)}, u32[]{:S(2)}) copy-start(f32[320]{0:T(512)} %param.24) | copy-start | bytes 3844
  428.6 190.3 %reduce-scatter.10.cloned.1.call-start = ((), (), s32[]{:S(2)}) async-start(), calls=%async_computation.8 | async-start | bytes 442368 | tf_op jit(solution)/shard_map/reduce_scatter | solution.py:61
  494.2 230.6 %all-gather.5.cloned.1.call-start = ((), (), s32[]{:S(2)}) async-start(), calls=%async_computation.9 | async-start | bytes 2949120 | tf_op jit(solution)/shard_map/all_gather | solution.py:170
  669.1 115.8 %all-gather.7.cloned.1.call-start = ((), (), s32[]{:S(2)}) async-start(), calls=%async_computation.12 | async-start | bytes 2949120 | tf_op jit(solution)/shard_map/all_gather | solution.py:171
  730.7 125.1 %copy-start.4 = (s32[256]{0:T(256)S(1)}, s32[256]{0:T(256)}, u32[]{:S(2)}) copy-start(s32[256]{0:T(256)} %param.27) | copy-start | bytes 3076
Sparse Core Ops, SparseCore 0:
  68.0 127.1 all-reduce.4
  202.0 70.0 reduce-scatter.5
  334.9 66.4 reduce-scatter.11
  403.8 66.7 reduce-scatter.7
  474.5 70.4 reduce-scatter.13
  548.8 70.0 reduce-scatter.9
  669.2 55.4 all-gather.4
  727.3 57.4 all-gather.6
where the time goes:
time: 927 us; the launch traced here: 926 us
  waiting for transfers between devices  512 us (55%)
  blocking collectives  354 us (38%)
  matrix products  28.1 us (3%)
  between operations  13.7 us (1%)
    psum x1, waiting for transfers between devices, per_device(): joint_sums = lax.psum(joint_part, 'col')  126 us
    reduce_scatter x2, waiting for transfers between devices, feed_forward(): lax.psum_scatter(jnp.dot(row_block, down_weight, preferred_element_type=j...  125 us
    reduce_scatter x2, waiting for transfers between devices, feed_forward(): lax.psum_scatter(jnp.dot(row_block, gate_up, preferred_element_type=jnp.f...  106 us
    reduce_scatter x1, waiting for transfers between devices, per_device(): lax.psum_scatter(jnp.dot(attn_all, w_out, preferred_element_type=jnp.floa...  66.2 us
    pmax x1, blocking collectives, per_device(): top_policy, top_refer = lax.pmax((policy_top, refer_top), ('row', 'col'))  65 us
    psum x1, blocking collectives, per_device(): lax.psum((policy_total * jnp.exp(policy_top - top_policy), refer_total *...  62.5 us
    psum x2, blocking collectives, rms_local(): grand_total = lax.psum(squares, 'col')  57.7 us
    all_gather x1, waiting for transfers between devices, per_device(): lax.all_gather(wide_pair[1], 'row', axis=0, tiled=True)  54.1 us
  transfers between devices with their start and end apart: 8, of which 8 were waited for; matrix products, arithmetic and copies ran while one was open for 2% of the time, Pallas kernels for 0%

commit v1 on v0

--- a/solution.py
+++ b/solution.py
@@ -98,7 +98,7 @@
     gathered = lax.all_gather(normed, "row", axis=0, tiled=True)
     w_joint = jnp.concatenate([w_query, w_key, w_value], axis=1)
     joint_part = jnp.dot(gathered, w_joint, preferred_element_type=jnp.float32)
-    joint_sums = lax.psum(joint_part, "col")
+    joint_sums = jnp.sum(lax.all_gather(joint_part, "col"), axis=0)
     token_index = jnp.arange(total_tokens, dtype=jnp.int32)
     segment, positions = sequence_layout(seq_lengths, token_index)
     angles = angles_for(positions, HEAD_DIM)

time: 927 us -> 891 us (0.961)
  waiting for transfers between devices: 512 us -> 469 us
    psum x1 -> x0, waiting for transfers between devices: 126 us -> none  [per_device(): joint_sums = lax.psum(joint_part, 'col')]
    all_gather x0 -> x1, waiting for transfers between devices: none -> 89.4 us  [per_device(): joint_sums = jnp.sum(lax.all_gather(joint_part, 'col'), axis=0)]
where the time goes in v1:
time: 891 us; the launch traced here: 890 us
  waiting for transfers between devices  469 us (53%)
  blocking collectives  358 us (40%)
  matrix products  27.1 us (3%)
  other arithmetic  15.1 us (2%)
  between operations  13.7 us (2%)
    reduce_scatter x2, waiting for transfers between devices, feed_forward(): lax.psum_scatter(jnp.dot(row_block, down_weight, preferred_element_type=j...  121 us
    reduce_scatter x2, waiting for transfers between devices, feed_forward(): lax.psum_scatter(jnp.dot(row_block, gate_up, preferred_element_type=jnp.f...  103 us
    all_gather x1, waiting for transfers between devices, per_device(): joint_sums = jnp.sum(lax.all_gather(joint_part, 'col'), axis=0)  89.4 us
    reduce_scatter x1, waiting for transfers between devices, per_device(): lax.psum_scatter(jnp.dot(attn_all, w_out, preferred_element_type=jnp.floa...  65.6 us
    pmax x1, blocking collectives, per_device(): top_policy, top_refer = lax.pmax((policy_top, refer_top), ('row', 'col'))  65 us
    psum x1, blocking collectives, per_device(): lax.psum((policy_total * jnp.exp(policy_top - top_policy), refer_total *...  62.5 us
    psum x2, blocking collectives, rms_local(): grand_total = lax.psum(squares, 'col')  57.7 us
    all_gather x1, waiting for transfers between devices, per_device(): lax.all_gather(wide_pair[1], 'row', axis=0, tiled=True)  53.9 us
  transfers between devices with their start and end apart: 8, of which 8 were waited for; matrix products, arithmetic and copies ran while one was open for 2% of the time, Pallas kernels for 0%

profile of v1, /device:TPU:1, one launch (start us, length us, event | category | flops | bytes accessed | tf_op | source)
XLA Modules:
  0.0 890.3 jit_solution(5126902512493316714)
XLA Ops:
  6.5 0.9 fusion.48
  7.5 28.6 %psum.56 = f32[32]{0:T(128)S(1)} all-reduce(f32[32]{0:T(128)S(1)} %fusion.48), channel_id=1, replica_groups=mesh['row'=8,'col'=16] {'col'}, use_global_device_ids=true, to_apply=%region_1.0 | all-reduce | flops 32 | bytes 256 | tf_op jit(solution)/shard_map/psum | solution.py:45
  36.1 0.8 fusion.50
  36.9 28.5 %all_gather.30 = bf16[256,320]{1,0:T(8,128)(2,1)S(1)} all-gather(bf16[32,320]{1,0:T(8,128)(2,1)S(1)} %fusion.50), channel_id=1, replica_groups=mesh['row'=8,'col'=16] {'row'}, dimensions={0}, use_global_device_ids=true | all-gather | bytes 184320 | tf_op jit(solution)/shard_map/all_gather | solution.py:98
  65.4 2.4 fusion.21
  68.3 0.5 multiply_cosine_fusion
  68.8 89.4 %all-gather.11.cloned.1.call-done = f32[4096,896]{1,0:T(8,128)} async-done(((f32[256,896]{1,0:T(8,128)}), f32[4096,896]{1,0:T(8,128)}) %all-gather.11.cloned.1.call-update) | async-done | bytes 14680080 | tf_op jit(solution)/shard_map/all_gather | solution.py:101
  158.2 5.9 reduce_sum.110
  164.2 0.2 copy.31
  164.5 0.2 copy.42
  164.8 0.2 copy.41
  165.0 0.6 fusion.47
  165.8 0.5 fusion.62
  166.2 0.2 fusion.10
  166.4 0.4 convolution_convert_fusion
  166.8 1.1 fusion.65
  168.0 4.0 slice_bitcast_fusion.2
  172.1 65.6 %reduce-scatter.6.cloned.1.call-done = f32[32,320]{1,0:T(8,128)} async-done(((f32[256,320]{1,0:T(8,128)}), f32[32,320]{1,0:T(8,128)}) %reduce-scatter.6.cloned.1.call-update) | async-done | bytes 40976 | tf_op jit(solution)/shard_map/reduce_scatter | solution.py:142
  237.7 0.8 fusion.51
  238.6 29.1 %psum.57 = f32[32]{0:T(128)S(1)} all-reduce(f32[32]{0:T(128)S(1)} %fusion.52), channel_id=1, replica_groups=mesh['row'=8,'col'=16] {'col'}, use_global_device_ids=true, to_apply=%region_10.11 | all-reduce | flops 32 | bytes 256 | tf_op jit(solution)/shard_map/psum | solution.py:45
  267.7 28.0 %all_gather.33 = bf16[256,320]{1,0:T(8,128)(2,1)S(1)} all-gather(bf16[32,320]{1,0:T(8,128)(2,1)S(1)} %fusion.54), channel_id=1, replica_groups=mesh['row'=8,'col'=16] {'row'}, dimensions={0}, use_global_device_ids=true | all-gather | bytes 184320 | tf_op jit(solution)/shard_map/all_gather | solution.py:151
  295.7 4.5 fusion
  300.3 2.9 fusion.4
  303.3 63.5 %reduce-scatter.8.cloned.1.call-done = f32[16,3456]{1,0:T(8,128)} async-done(((f32[256,3456]{1,0:T(8,128)}), f32[16,3456]{1,0:T(8,128)}) %reduce-scatter.8.cloned.1.call-update) | async-done | bytes 221200 | tf_op jit(solution)/shard_map/reduce_scatter | solution.py:52
  366.8 1.1 fusion.40
  367.9 26.2 %all_gather.34 = bf16[256,1728]{1,0:T(8,128)(2,1)S(1)} all-gather(bf16[16,1728]{1,0:T(8,128)(2,1)S(1)} %fusion.40), channel_id=1, replica_groups=mesh['row'=8,'col'=16] {'col'}, dimensions={0}, use_global_device_ids=true | all-gather | bytes 940032 | tf_op jit(solution)/shard_map/all_gather | solution.py:59
  394.1 1.4 fusion.13
  395.5 39.9 %reduce-scatter.12.cloned.1.call-done = f32[16,3456]{1,0:T(8,128)} async-done(((f32[256,3456]{1,0:T(8,128)}), f32[16,3456]{1,0:T(8,128)}) %reduce-scatter.12.cloned.1.call-update) | async-done | bytes 221200 | tf_op jit(solution)/shard_map/reduce_scatter | solution.py:52
  435.5 1.1 fusion.39
  436.6 23.9 %all_gather.37 = bf16[256,1728]{1,0:T(8,128)(2,1)S(1)} all-gather(bf16[16,1728]{1,0:T(8,128)(2,1)S(1)} %fusion.39), channel_id=1, replica_groups=mesh['row'=8,'col'=16] {'col'}, dimensions={0}, use_global_device_ids=true | all-gather | bytes 940032 | tf_op jit(solution)/shard_map/all_gather | solution.py:59
  460.4 1.4 fusion.11
  461.9 47.7 %reduce-scatter.10.cloned.1.call-done = f32[32,320]{1,0:T(8,128)} async-done(((f32[256,320]{1,0:T(8,128)}), f32[32,320]{1,0:T(8,128)}) %reduce-scatter.10.cloned.1.call-update) | async-done | bytes 40976 | tf_op jit(solution)/shard_map/reduce_scatter | solution.py:61
  509.7 73.5 %reduce-scatter.14.cloned.1.call-done = f32[32,320]{1,0:T(8,128)} async-done(((f32[256,320]{1,0:T(8,128)}), f32[32,320]{1,0:T(8,128)}) %reduce-scatter.14.cloned.1.call-update) | async-done | bytes 40976 | tf_op jit(solution)/shard_map/reduce_scatter | solution.py:61
  583.2 0.9 multiply_reduce_fusion.1
  584.1 29.1 %all-reduce.2 = (f32[32]{0:T(128)S(1)}, f32[32]{0:T(128)S(1)}) all-reduce(f32[32]{0:T(128)S(1)} %get-tuple-element.30, f32[32]{0:T(128)S(1)} %get-tuple-element.28), channel_id=1, replica_groups=mesh['row'=8,'col'=16] {'col'}, use_global_device_ids=true, to_apply=%region_24.25 | all-reduce | flops 64 | bytes 512 | tf_op jit(solution)/shard_map/psum | solution.py:156
  613.2 0.9 fusion.55
  614.1 18.1 %all-gather.1 = bf16[16,320,32]{1,2,0:T(8,128)(2,1)S(1)} all-gather(bf16[1,320,32]{1,2,0:T(8,128)(2,1)S(1)} %get-tuple-element.52), channel_id=1, replica_groups=mesh['row'=8,'col'=16] {'col'}, dimensions={0}, use_global_device_ids=true | all-gather | bytes 348160 | tf_op jit(solution)/shard_map/all_gather | solution.py:166
  632.3 1.0 reshape.256
  633.4 19.3 %all-gather.2 = bf16[16,320,32]{1,2,0:T(8,128)(2,1)S(1)} all-gather(bf16[1,320,32]{1,2,0:T(8,128)(2,1)S(1)} %get-tuple-element.53), channel_id=1, replica_groups=mesh['row'=8,'col'=16] {'col'}, dimensions={0}, use_global_device_ids=true | all-gather | bytes 348160 | tf_op jit(solution)/shard_map/all_gather | solution.py:167
  652.8 1.0 reshape.258
  653.9 35.0 %all-gather.7.cloned.1.call-done = bf16[256,5120]{1,0:T(8,128)(2,1)} async-done(((bf16[32,5120]{1,0:T(8,128)(2,1)}), bf16[256,5120]{1,0:T(8,128)(2,1)}) %all-gather.7.cloned.1.call-update) | async-done | bytes 2621456 | tf_op jit(solution)/shard_map/all_gather | solution.py:170
  688.9 5.9 fusion.63
  694.9 53.9 %all-gather.9.cloned.1.call-done = bf16[256,5120]{1,0:T(8,128)(2,1)} async-done(((bf16[32,5120]{1,0:T(8,128)(2,1)}), bf16[256,5120]{1,0:T(8,128)(2,1)}) %all-gather.9.cloned.1.call-update) | async-done | bytes 2621456 | tf_op jit(solution)/shard_map/all_gather | solution.py:171
  748.7 5.9 fusion.64
  754.7 65.0 %all-reduce.1 = (f32[256]{0:T(256)S(1)}, f32[256]{0:T(256)S(1)}) all-reduce(f32[256]{0:T(256)S(1)} %get-tuple-element.62, f32[256]{0:T(256)S(1)} %get-tuple-element.60), channel_id=1, replica_groups=mesh['row'=8,'col'=16] {'row','col'}, use_global_device_ids=true, to_apply=%region_28.29 | all-reduce | flops 512 | bytes 4096 | tf_op jit(solution)/shard_map/pmax | solution.py:187
  819.6 0.5 exponential_reduce_fusion.1
  820.1 62.5 %all-reduce = (f32[256]{0:T(256)S(1)}, f32[256]{0:T(256)S(1)}, f32[256]{0:T(256)S(1)}, f32[256]{0:T(256)S(1)}) all-reduce(f32[256]{0:T(256)S(1)} %get-tuple-element.54, f32[256]{0:T(256)S(1)} %exponential_multiply_fusion, f32[256]{0:T(256)S(1)} %get-tuple-element.18, ...), channel_id=1, replica_groups=mesh['row'=8,'col'=16] {'row','col'}, use_global_device_ids=true, to_apply=%region_26.27 | all-reduce | flops 1024 | bytes 8192 | tf_op jit(solution)/shard_map/psum | solution.py:188
  882.7 0.8 fusion.17
  (51 shorter events, 1.6 us)
Async XLA Ops:
  6.5 160.3 %copy-start = (bf16[640,320]{0,1:T(8,128)(2,1)S(1)}, bf16[640,320]{0,1:T(8,128)(2,1)}, u32[]{:S(2)}) copy-start(bf16[640,320]{0,1:T(8,128)(2,1)} %param.19) | copy-start | bytes 1228804
  6.5 61.3 %copy-start.5 = (s32[8]{0:T(128)S(1)}, s32[8]{0:T(128)}, u32[]{:S(2)}) copy-start(s32[8]{0:T(128)} %param.26) | copy-start | bytes 100
  6.5 151.7 %all-gather.11.cloned.1.call-start = ((), (), s32[]{:S(2)}) async-start(), calls=%async_computation.12 | async-start | bytes 15597568 | tf_op jit(solution)/shard_map/all_gather | solution.py:101
  67.8 169.8 %reduce-scatter.6.cloned.1.call-start = ((), (), s32[]{:S(2)}) async-start(), calls=%async_computation.5 | async-start | bytes 442368 | tf_op jit(solution)/shard_map/reduce_scatter | solution.py:142
  168.0 69.7 %copy-start.1 = (bf16[32,320]{1,0:T(8,128)(2,1)S(1)}, bf16[32,320]{1,0:T(8,128)(2,1)}, u32[]{:S(2)}) copy-start(bf16[32,320]{1,0:T(8,128)(2,1)} %param.14) | copy-start | bytes 61444
  168.0 99.7 %copy-start.3 = (f32[320]{0:T(512)S(1)}, f32[320]{0:T(512)}, u32[]{:S(2)}) copy-start(f32[320]{0:T(512)} %param.20) | copy-start | bytes 3844
  168.0 198.8 %reduce-scatter.8.cloned.1.call-start = ((), (), s32[]{:S(2)}) async-start(), calls=%async_computation.6 | async-start | bytes 3760128 | tf_op jit(solution)/shard_map/reduce_scatter | solution.py:52
  300.2 135.3 %reduce-scatter.12.cloned.1.call-start = ((), (), s32[]{:S(2)}) async-start(), calls=%async_computation.9 | async-start | bytes 3760128 | tf_op jit(solution)/shard_map/reduce_scatter | solution.py:52
  303.2 90.9 %copy-start.6 = (bf16[2,1728,320]{1,2,0:T(8,128)(2,1)S(1)}, bf16[2,1728,320]{1,2,0:T(8,128)(2,1)}, u32[]{:S(2)}) copy-start(bf16[2,1728,320]{1,2,0:T(8,128)(2,1)} %param.23) | copy-start | bytes 6635524
  303.2 206.4 %reduce-scatter.10.cloned.1.call-start = ((), (), s32[]{:S(2)}) async-start(), calls=%async_computation.7 | async-start | bytes 442368 | tf_op jit(solution)/shard_map/reduce_scatter | solution.py:61
  395.5 217.7 %copy-start.2 = (f32[320]{0:T(512)S(1)}, f32[320]{0:T(512)}, u32[]{:S(2)}) copy-start(f32[320]{0:T(512)} %param.24) | copy-start | bytes 3844
  395.5 187.7 %reduce-scatter.14.cloned.1.call-start = ((), (), s32[]{:S(2)}) async-start(), calls=%async_computation.10 | async-start | bytes 442368 | tf_op jit(solution)/shard_map/reduce_scatter | solution.py:61
  461.9 227.0 %all-gather.7.cloned.1.call-start = ((), (), s32[]{:S(2)}) async-start(), calls=%async_computation.8 | async-start | bytes 2949120 | tf_op jit(solution)/shard_map/all_gather | solution.py:170
  633.3 115.4 %all-gather.9.cloned.1.call-start = ((), (), s32[]{:S(2)}) async-start(), calls=%async_computation.11 | async-start | bytes 2949120 | tf_op jit(solution)/shard_map/all_gather | solution.py:171
  694.8 124.8 %copy-start.4 = (s32[256]{0:T(256)S(1)}, s32[256]{0:T(256)}, u32[]{:S(2)}) copy-start(s32[256]{0:T(256)} %param.27) | copy-start | bytes 3076
Sparse Core Ops, SparseCore 0:
  68.0 90.2 all-gather.10
  168.1 69.5 reduce-scatter.5
  300.3 66.3 reduce-scatter.7
  369.1 66.3 reduce-scatter.11
  438.9 70.6 reduce-scatter.9
  513.1 70.0 reduce-scatter.13
  633.5 55.4 all-gather.6
  691.2 57.4 all-gather.8
